TPU v7x, 256 devices: a whole 4x4x8 slice. The times are simulated.
256 devices in a mesh: traj: 32 (over z, y), seg: 8 (over x, core).
Axes of the slice: x: 4, y: 4, z: 8, core: 2. Of those that a mesh axis runs over, the one named last changes fastest.
Arguments:
- coords: float32 [32, 1024, 3, 512], P('traj', 'seg')
- pairs: int32 [2, 1024], replicated, may hold values from 0 to 511, as said below
- lengths: int32 [32], P('traj'), may hold values from 1 to 1024, 24576 in all
Outputs:
- projected: float32 [32, 1024, 128], P('traj', 'seg')
Inputs may be any that keep to these rules, and one draw needn't show every extreme that they name: `pairs`: atom indices; the two atoms of a contact differ. `lengths`: each trajectory's recorded frames fill its first slots.
All inputs are finite; a program needn't handle non-finite values. No bound on the sum of `lengths` on one device may be relied on, other than what follows from the above.
Results may differ from a plain program's by a relative error of at most 0.0003.
Values sent between devices are 32-bit elements; how exact they have to be, the bound alone decides.
No kernel may reach another device: no remote copies, remote signals or barrier semaphores. Data moves between devices by JAX's collectives and lax.ppermute only.
A program may use at most 128 MiB of HBM per device.

v0:
```python
import jax
import jax.numpy as jnp
from jax import lax
from jax.sharding import PartitionSpec as P

K = 128
LAG = 10
ITERS = 3
exact_mode = lax.Precision.HIGHEST
soft_square = 0.1
ridge_term = 0.01
spectral_shift = 2.0


def from_behind(x, axis, by):
    peers = lax.axis_size(axis)
    pairs = [(i, i + by) for i in range(peers) if 0 <= i + by < peers]
    return lax.ppermute(x, axis, pairs)


def featurize(frames, pairs):
    first_atom = jnp.take(frames, pairs[0], axis=2)
    second_atom = jnp.take(frames, pairs[1], axis=2)
    offset = first_atom - second_atom
    return jnp.sqrt(jnp.sum(offset * offset, axis=1) + soft_square)


def tri_solve(factor, rhs, transposed):
    return lax.linalg.triangular_solve(
        factor, rhs, left_side=True, lower=True, transpose_a=transposed
    )


def cross_gram(left_rows, right_rows):
    return lax.dot_general(
        left_rows,
        right_rows,
        (((0,), (0,)), ((), ())),
        precision=exact_mode,
        preferred_element_type=jnp.float32,
    )


def row_sum(weights, matrix):
    return jnp.dot(weights, matrix, precision=exact_mode, preferred_element_type=jnp.float32)


def subspace(c_zero, c_lag, basis_width):
    lower_factor = jnp.linalg.cholesky(c_zero)
    identity = jnp.eye(c_zero.shape[0], dtype=jnp.float32)
    basis_q = identity[:, :basis_width]
    for sweep in range(ITERS):
        inner_solve = tri_solve(lower_factor, basis_q, True)
        moved_block = jnp.dot(
            c_lag, inner_solve, precision=exact_mode, preferred_element_type=jnp.float32
        )
        image_block = tri_solve(lower_factor, moved_block, False) + spectral_shift * basis_q
        gram_small = cross_gram(image_block, image_block)
        small_factor = jnp.linalg.cholesky(gram_small)
        basis_q = tri_solve(small_factor, image_block.T, False).T
    return tri_solve(lower_factor, basis_q, True)


def on_device(coords, pairs, lengths):
    frames = coords[0]
    frame_rows = frames.shape[0]
    features = featurize(frames, pairs)
    feature_count = features.shape[1]
    frame_index = lax.axis_index("seg") * frame_rows + jnp.arange(frame_rows, dtype=jnp.int32)
    length = lengths[0]
    is_valid = (frame_index < length).astype(jnp.float32)
    paired = (frame_index + LAG < length).astype(jnp.float32)
    arriving = from_behind(features[:LAG], "seg", -1)
    lagged = jnp.concatenate([features[LAG:], arriving], axis=0)
    count_all = jnp.sum(is_valid)
    count_pair = jnp.sum(paired)
    sum_all = row_sum(is_valid, features)
    sum_lead = row_sum(paired, features)
    sum_ahead = row_sum(paired, lagged)
    own_counts = jnp.stack([count_all, count_pair])[None, :]
    own_totals = jnp.stack([sum_all, sum_lead, sum_ahead])[None]
    all_counts, all_totals = (
        lax.all_gather(own_counts, ("traj", "seg"), axis=0, tiled=True),
        lax.all_gather(own_totals, ("traj", "seg"), axis=0, tiled=True),
    )
    frames_total = jnp.sum(all_counts[:, 0])
    pairs_total = jnp.sum(all_counts[:, 1])
    mean_all = jnp.sum(all_totals[:, 0], axis=0) / frames_total
    mean_lead = jnp.sum(all_totals[:, 1], axis=0) / pairs_total
    mean_ahead = jnp.sum(all_totals[:, 2], axis=0) / pairs_total
    center_all = sum_all / jnp.maximum(count_all, 1.0)
    center_lead = sum_lead / jnp.maximum(count_pair, 1.0)
    center_ahead = sum_ahead / jnp.maximum(count_pair, 1.0)
    centered = (features - center_all) * is_valid[:, None]
    lead_rows = (features - center_lead) * paired[:, None]
    ahead_rows = (lagged - center_ahead) * paired[:, None]
    gram_zero = cross_gram(centered, centered)
    gram_lag = cross_gram(lead_rows, ahead_rows)
    total_zero, total_lag = lax.psum((gram_zero, gram_lag), ("traj", "seg"))
    symmetric_lag = total_lag + total_lag.T
    safe_counts = jnp.maximum(all_counts, 1.0)
    spread_all = all_totals[:, 0] / safe_counts[:, 0:1] - mean_all
    spread_lead = all_totals[:, 1] / safe_counts[:, 1:2] - mean_lead
    spread_ahead = all_totals[:, 2] / safe_counts[:, 1:2] - mean_ahead
    total_zero = total_zero + cross_gram(spread_all * all_counts[:, 0:1], spread_all)
    between_lag = cross_gram(spread_lead * all_counts[:, 1:2], spread_ahead)
    symmetric_lag = symmetric_lag + between_lag + between_lag.T
    identity = jnp.eye(feature_count, dtype=jnp.float32)
    c_zero = total_zero / frames_total + ridge_term * identity
    c_lag = symmetric_lag / (2.0 * pairs_total)
    basis = subspace(c_zero, c_lag, K)
    shifted = (features - mean_all) * is_valid[:, None]
    projected = jnp.dot(shifted, basis, precision=exact_mode, preferred_element_type=jnp.float32)
    return projected[None]


def solution(mesh):
    return jax.shard_map(
        on_device,
        mesh=mesh,
        in_specs=(P("traj", "seg", None, None), P(), P("traj")),
        out_specs=P("traj", "seg", None),
        check_vma=False,
    )
```

profile of v0, /device:TPU:1, one launch (start us, length us, event | category | flops | bytes accessed | tf_op | source)
XLA Modules:
  0.0 1033.5 jit_solution(3482435308951660966)
XLA Ops:
  8.9 3.6 gather_fusion
  12.5 8.0 gather_fusion.1
  20.4 7.7 fusion.4
  28.3 5.1 collective-permute-start
  37.6 5.6 fusion.27
  43.9 5.6 fusion.22
  51.7 80.3 %all-reduce.1 = f32[512]{0:T(512)S(1)} all-reduce(f32[512]{0:T(512)S(1)} %maximum_dynamic-update-slice_fusion), channel_id=3, replica_groups=mesh['traj'=32,'seg'=8] {'traj','seg'}, use_global_device_ids=true, to_apply=%add.1 | all-reduce | flops 512 | bytes 4096
  136.0 193.8 %all-reduce.5.cloned.1.call-done = (f32[1024,1024]{1,0:T(8,128)}, f32[1024,1024]{0,1:T(8,128)}) async-done(((f32[1024,1024]{1,0:T(8,128)}, f32[1024,1024]{0,1:T(8,128)}), (f32[1024,1024]{1,0:T(8,128)}, f32[1024,1024]{0,1:T(8,128)})) %all-reduce.5.cloned.1.call-update) | async-done | bytes 8388624 | tf_op jit(solution)/shard_map/psum | solution.py:99
  329.7 5.3 copy.134
  335.1 115.0 %all-gather.5.cloned.1.call-done = f32[256,3,1024]{2,1,0:T(4,128)} async-done(((f32[1,3,1024]{2,1,0:T(4,128)}), f32[256,3,1024]{2,1,0:T(4,128)}) %all-gather.5.cloned.1.call-update) | async-done | bytes 3145744 | tf_op jit(solution)/shard_map/all_gather | solution.py:84
  450.1 6.1 slice_reduce_fusion.2
  457.8 9.7 broadcast_multiply_fusion
  467.5 6.7 select_add_fusion
  474.1 5.5 copy.116
  479.7 4.4 fusion.2
  486.1 11.7 %cholesky.236 = f32[128,128]{1,0:T(8,128)S(1)} custom-call(f32[128,128]{1,0:T(8,128)S(1)} %cholesky.667), custom_call_target="Cholesky" | custom-call | tf_op jit(solution)/shard_map/jit(cholesky)/cholesky | solution.py:49
  497.8 9.8 custom-call.70
  511.5 11.7 %cholesky.259 = f32[128,128]{1,0:T(8,128)S(1)} custom-call(f32[128,128]{1,0:T(8,128)S(1)} %cholesky.671), custom_call_target="Cholesky" | custom-call | tf_op jit(solution)/shard_map/jit(cholesky)/cholesky | solution.py:49
  527.1 9.8 custom-call.71
  543.5 11.7 %cholesky.493 = f32[128,128]{1,0:T(8,128)S(1)} custom-call(f32[128,128]{1,0:T(8,128)S(1)} %cholesky.676), custom_call_target="Cholesky" | custom-call | tf_op jit(solution)/shard_map/jit(cholesky)/cholesky | solution.py:49
  556.0 9.8 custom-call.72
  567.0 3.5 convolution_subtract_fusion.2
  570.6 11.7 %cholesky.512 = f32[128,128]{1,0:T(8,128)S(1)} custom-call(f32[128,128]{1,0:T(8,128)S(1)} %cholesky.681), custom_call_target="Cholesky" | custom-call | tf_op jit(solution)/shard_map/jit(cholesky)/cholesky | solution.py:49
  583.1 9.8 custom-call.73
  594.0 3.2 convolution_subtract_fusion.3
  597.2 11.9 %cholesky.531 = f32[128,128]{1,0:T(8,128)S(1)} custom-call(f32[128,128]{1,0:T(8,128)S(1)} %cholesky.686), custom_call_target="Cholesky" | custom-call | tf_op jit(solution)/shard_map/jit(cholesky)/cholesky | solution.py:49
  609.8 9.8 custom-call.74
  620.8 3.1 convolution_subtract_fusion.4
  623.9 11.7 %cholesky.551 = f32[128,128]{1,0:T(8,128)S(1)} custom-call(f32[128,128]{1,0:T(8,128)S(1)} %cholesky.691), custom_call_target="Cholesky" | custom-call | tf_op jit(solution)/shard_map/jit(cholesky)/cholesky | solution.py:49
  636.3 9.8 custom-call.75
  650.0 11.7 %cholesky.571 = f32[128,128]{1,0:T(8,128)S(1)} custom-call(f32[128,128]{1,0:T(8,128)S(1)} %cholesky.696), custom_call_target="Cholesky" | custom-call | tf_op jit(solution)/shard_map/jit(cholesky)/cholesky | solution.py:49
  662.5 9.8 custom-call.76
  675.3 11.7 %cholesky.589 = f32[128,128]{1,0:T(8,128)S(1)} custom-call(f32[128,128]{1,0:T(8,128)S(1)} %convolution_subtract_fusion.41), custom_call_target="Cholesky" | custom-call | tf_op jit(solution)/shard_map/jit(cholesky)/cholesky | solution.py:49
  697.9 4.9 select_select_fusion
  702.8 28.7 %while.14 = (s32[]{:T(128)}, f32[1024,1024]{0,1:T(8,128)}, s32[8,2]{0,1:T(2,128)S(1)}, f32[8,128,128]{2,1,0:T(8,128)}, s32[]{:T(128)}) while((s32[]{:T(128)}, f32[1024,1024]{0,1:T(8,128)}, s32[8,2]{0,1:T(2,128)S(1)}, f32[8,128,128]{2,1,0:T(8,128)}, s32[]{:T(128)}) %tuple.152), condition=%wide.while_cond.clone.2, body=%wide.while_body.clone.2.sunk | while | flops 2 | bytes 393829 | solution.py:29
  731.5 79.8 %custom-call.93 = f32[8,128,128]{1,2,0:T(8,128)S(1)} custom-call(f32[8,128,128]{2,1,0:T(8,128)} %get-tuple-element.62), custom_call_target="InvertDiagBlocksLowerTriangular" | custom-call | tf_op jit(solution)/shard_map/triangular_solve/custom-call.16 | solution.py:29
  826.3 5.2 fusion.6
  831.5 5.5 copy.135
  837.0 7.9 fusion
  846.9 3.4 fusion.333
  866.1 11.7 %cholesky.636 = f32[128,128]{1,0:T(8,128)S(1)} custom-call(f32[128,128]{1,0:T(8,128)S(1)} %fusion.231), custom_call_target="Cholesky" | custom-call | tf_op jit(solution)/shard_map/jit(cholesky)/cholesky | solution.py:59
  879.2 9.8 custom-call.86
  904.0 3.8 fusion.334
  923.9 11.9 %cholesky.647 = f32[128,128]{1,0:T(8,128)S(1)} custom-call(f32[128,128]{1,0:T(8,128)S(1)} %fusion.229), custom_call_target="Cholesky" | custom-call | tf_op jit(solution)/shard_map/jit(cholesky)/cholesky | solution.py:59
  937.1 9.8 custom-call.89
  961.1 3.7 fusion.335
  987.3 11.7 %cholesky.658 = f32[128,128]{1,0:T(8,128)S(1)} custom-call(f32[128,128]{1,0:T(8,128)S(1)} %fusion.227), custom_call_target="Cholesky" | custom-call | tf_op jit(solution)/shard_map/jit(cholesky)/cholesky | solution.py:59
  1000.3 10.0 custom-call.92
  (409 shorter events, 196.3 us)
Async XLA Ops:
  6.5 323.2 %all-reduce.5.cloned.1.call-start = ((), (), s32[]{:S(2)}) async-start(), calls=%async_computation.1 | async-start | bytes 16777216 | tf_op jit(solution)/shard_map/psum | solution.py:99
  28.3 15.2 %collective-permute-start = (f32[10,1024]{0,1:T(8,128)S(1)}, f32[10,1024]{0,1:T(8,128)S(1)}, u32[]{:S(2)}, u32[]{:S(2)}) collective-permute-start(f32[10,1024]{0,1:T(8,128)S(1)} %bitcast.438), channel_id=1, source_target_pairs={{1,0},{2,1},{3,2},{4,3},{5,4},{6,5},{7,6},{9,8},{10,9},{11,10},{12... | collective-permute-start | bytes 122888 | tf_op jit(solution)/shard_map/ppermute | solution.py:18
  49.6 400.6 %all-gather.5.cloned.1.call-start = ((), (), s32[]{:S(2)}) async-start(), calls=%async_computation | async-start | bytes 4210688 | tf_op jit(solution)/shard_map/all_gather | solution.py:84
  134.1 1.0 copy-start.6
  456.2 11.3 %copy-start.11 = (f32[1024,1024]{0,1:T(8,128)S(1)}, f32[1024,1024]{0,1:T(8,128)}, u32[]{:S(2)}) copy-start(f32[1024,1024]{0,1:T(8,128)} %get-tuple-element.165) | copy-start | bytes 12582916
  484.1 2.0 copy-start.3
  510.7 0.8 copy-start.5
  524.4 12.6 %copy-start.4 = (f32[896,128]{0,1:T(8,128)S(1)}, f32[896,128]{0,1:T(8,128)}, u32[]{:S(2)}) copy-start(f32[896,128]{0,1:T(8,128)} %copy.118) | copy-start | bytes 1376260
  825.5 0.8 copy-start.7
  837.0 9.9 copy-start.8
  844.9 1.9 copy-start
  893.4 10.5 %copy-start.1 = (f32[1024,1024]{1,0:T(8,128)S(1)}, f32[1024,1024]{1,0:T(8,128)}, u32[]{:S(2)}) copy-start(f32[1024,1024]{1,0:T(8,128)} %copy-done) | copy-start | bytes 12582916
  912.8 0.7 copy-start.9
  950.5 10.5 %copy-start.2 = (f32[1024,1024]{1,0:T(8,128)S(1)}, f32[1024,1024]{1,0:T(8,128)}, u32[]{:S(2)}) copy-start(f32[1024,1024]{1,0:T(8,128)} %copy-done) | copy-start | bytes 12582916
  972.6 13.6 %copy-start.10 = (f32[128,128]{0,1:T(8,128)S(1)}, f32[128,128]{0,1:T(8,128)}, u32[]{:S(2)}) copy-start(f32[128,128]{0,1:T(8,128)} %copy.183) | copy-start | bytes 196612
Sparse Core Ops, SparseCore 0:
  49.7 280.0 all-reduce.4
  333.3 116.7 all-gather.4
where the time goes:
time: 1040 us; the launch traced here: 1030 us
  other arithmetic  364 us (35%)
  waiting for transfers between devices  309 us (30%)
  matrix products  166 us (16%)
  local copies, waits for them, and re-layouts  85.1 us (8%)
  blocking collectives  80.3 us (8%)
  between operations  23.4 us (2%)
    psum x1, waiting for transfers between devices, on_device(): total_zero, total_lag = lax.psum((gram_zero, gram_lag), ('traj', 'seg'))  194 us
    another operation x31, other arithmetic, subspace(): lower_factor = jnp.linalg.cholesky(c_zero)  168 us
    another operation x10, other arithmetic, tri_solve(): lax.linalg.triangular_solve(factor, rhs, left_side=True, lower=True, tran...  116 us
    all_gather x1, waiting for transfers between devices, on_device(): lax.all_gather(own_totals, ('traj', 'seg'), axis=0, tiled=True)  115 us
    another operation x108, matrix products, tri_solve(): lax.linalg.triangular_solve(factor, rhs, left_side=True, lower=True, tran...  97.6 us
    unnamed x1, blocking collectives  80.3 us
    another operation x9, other arithmetic, subspace(): small_factor = jnp.linalg.cholesky(gram_small)  37.3 us
    another operation x78, local copies, waits for them, and re-layouts, tri_solve(): lax.linalg.triangular_solve(factor, rhs, left_side=True, lower=True, tran...  34 us
  transfers between devices with their start and end apart: 3, of which 2 were waited for; matrix products, arithmetic and copies ran while one was open for 2% of the time, Pallas kernels for 0%

commit v1 on v0

--- a/solution.py
+++ b/solution.py
@@ -1,3 +1,4 @@
+import functools
 import jax
 import jax.numpy as jnp
 from jax import lax
@@ -10,6 +11,15 @@
 soft_square = 0.1
 ridge_term = 0.01
 spectral_shift = 2.0
+
+
+def carry_hubs_now(raw, axis_key, peer_axis):
+    for p in (axis_key, peer_axis):
+        raw = jax.lax.psum(raw, p)
+    return raw
+
+
+drive_column = functools.partial(carry_hubs_now, axis_key="traj", peer_axis="seg")
 
 
 def from_behind(x, axis, by):
@@ -96,7 +106,7 @@
     ahead_rows = (lagged - center_ahead) * paired[:, None]
     gram_zero = cross_gram(centered, centered)
     gram_lag = cross_gram(lead_rows, ahead_rows)
-    total_zero, total_lag = lax.psum((gram_zero, gram_lag), ("traj", "seg"))
+    total_zero, total_lag = drive_column((gram_zero, gram_lag))
     symmetric_lag = total_lag + total_lag.T
     safe_counts = jnp.maximum(all_counts, 1.0)
     spread_all = all_totals[:, 0] / safe_counts[:, 0:1] - mean_all

time: 1040 us -> 956 us (0.919)
  waiting for transfers between devices: 309 us -> 210 us
    all_gather x1, waiting for transfers between devices: 115 us -> 0.03 us  [on_device(): lax.all_gather(own_totals, ('traj', 'seg'), axis=0, tiled=True)]
    psum x1 -> x2, waiting for transfers between devices: 194 us -> 210 us  [carry_hubs_now(): raw = jax.lax.psum(raw, p)]
  transfers between devices with their start and end apart: 3 -> 4, of which waited for: 2 -> 2; matrix products, arithmetic and copies ran while one was open for 2% -> 4% of each run, Pallas kernels for 0% -> 0%
where the time goes in v1:
time: 956 us; the launch traced here: 947 us
  other arithmetic  366 us (38%)
  waiting for transfers between devices  210 us (22%)
  matrix products  169 us (18%)
  local copies, waits for them, and re-layouts  89.9 us (9%)
  blocking collectives  82 us (9%)
  between operations  24.7 us (3%)
    psum x2, waiting for transfers between devices, carry_hubs_now(): raw = jax.lax.psum(raw, p)  210 us
    another operation x31, other arithmetic, subspace(): lower_factor = jnp.linalg.cholesky(c_zero)  170 us
    another operation x10, other arithmetic, tri_solve(): lax.linalg.triangular_solve(factor, rhs, left_side=True, lower=True, tran...  116 us
    another operation x108, matrix products, tri_solve(): lax.linalg.triangular_solve(factor, rhs, left_side=True, lower=True, tran...  99.4 us
    unnamed x1, blocking collectives  82 us
    another operation x9, other arithmetic, subspace(): small_factor = jnp.linalg.cholesky(gram_small)  37.3 us
    another operation x78, local copies, waits for them, and re-layouts, tri_solve(): lax.linalg.triangular_solve(factor, rhs, left_side=True, lower=True, tran...  35.1 us
    dot_general x7, matrix products, cross_gram(): lax.dot_general(left_rows, right_rows, (((0,), (0,)), ((), ())), precisio...  28.1 us
  transfers between devices with their start and end apart: 4, of which 2 were waited for; matrix products, arithmetic and copies ran while one was open for 4% of the time, Pallas kernels for 0%

profile of v1, /device:TPU:1, one launch (start us, length us, event | category | flops | bytes accessed | tf_op | source)
XLA Modules:
  0.0 947.1 jit_solution(4647347559392322370)
XLA Ops:
  9.7 8.0 gather_fusion
  17.7 8.0 gather_fusion.1
  25.7 8.5 fusion.4
  34.3 5.1 collective-permute-start
  43.7 5.6 fusion.27
  50.0 5.6 fusion.22
  57.8 82.0 %all-reduce.1 = f32[512]{0:T(512)S(1)} all-reduce(f32[512]{0:T(512)S(1)} %maximum_dynamic-update-slice_fusion), channel_id=3, replica_groups=mesh['traj'=32,'seg'=8] {'traj','seg'}, use_global_device_ids=true, to_apply=%add.1 | all-reduce | flops 512 | bytes 4096
  142.4 128.1 %all-reduce.7.cloned.1.call-done = (f32[1024,1024]{1,0:T(8,128)}, f32[1024,1024]{0,1:T(8,128)}) async-done(((f32[1024,1024]{1,0:T(8,128)}, f32[1024,1024]{0,1:T(8,128)}), (f32[1024,1024]{1,0:T(8,128)}, f32[1024,1024]{0,1:T(8,128)})) %all-reduce.7.cloned.1.call-update) | async-done | bytes 8388624 | tf_op jit(solution)/shard_map/psum | solution.py:18
  270.6 6.0 slice_reduce_fusion.2
  277.9 9.9 %broadcast_multiply_fusion = (f32[256,1,1024]{2,1,0:T(1,128)}, f32[256,1,1024]{2,1,0:T(1,128)}, f32[256,1,1024]{2,1,0:T(1,128)S(1)}, f32[256,1,1024]{2,1,0:T(1,128)S(1)}) fusion(f32[256]{0:T(256)S(1)} %get-tuple-element.150, f32[1024]{0:T(1024)S(1)} %broadcast_divide_fusion.5, f32[256]{0:T(256)S(1)} %get-tuple-element.154, ...), kind=kLoop, calls=%fused_computation.110 | loop fusion | flops 2097152 | bytes 7356416 | tf_op jit(solution)/shard_map/mul | solution.py:115
  287.8 5.2 fusion.6
  293.0 5.4 copy.135
  298.4 82.2 %all-reduce.9.cloned.1.call-done = (f32[1024,1024]{1,0:T(8,128)}, f32[1024,1024]{0,1:T(8,128)}) async-done(((f32[1024,1024]{1,0:T(8,128)}, f32[1024,1024]{0,1:T(8,128)}), (f32[1024,1024]{1,0:T(8,128)}, f32[1024,1024]{0,1:T(8,128)})) %all-reduce.9.cloned.1.call-update) | async-done | bytes 8388624 | tf_op jit(solution)/shard_map/psum | solution.py:18
  380.6 9.3 select_add_fusion
  389.9 5.5 copy.116
  395.4 4.4 fusion.2
  401.9 11.7 %cholesky.236 = f32[128,128]{1,0:T(8,128)S(1)} custom-call(f32[128,128]{1,0:T(8,128)S(1)} %cholesky.667), custom_call_target="Cholesky" | custom-call | tf_op jit(solution)/shard_map/jit(cholesky)/cholesky | solution.py:59
  413.6 9.8 %custom-call.70 = f32[1,128,128]{1,2,0:T(8,128)S(1)} custom-call(f32[1,128,128]{2,1,0:T(8,128)S(1)} %get-tuple-element.244), custom_call_target="InvertDiagBlocksLowerTriangular" | custom-call | tf_op jit(solution)/shard_map/jit(cholesky)/cholesky | solution.py:59
  426.5 11.7 %cholesky.259 = f32[128,128]{1,0:T(8,128)S(1)} custom-call(f32[128,128]{1,0:T(8,128)S(1)} %cholesky.671), custom_call_target="Cholesky" | custom-call | tf_op jit(solution)/shard_map/jit(cholesky)/cholesky | solution.py:59
  442.8 10.6 %custom-call.71 = f32[1,128,128]{1,2,0:T(8,128)S(1)} custom-call(f32[1,128,128]{2,1,0:T(8,128)} %get-tuple-element.242), custom_call_target="InvertDiagBlocksLowerTriangular" | custom-call | tf_op jit(solution)/shard_map/jit(cholesky)/cholesky | solution.py:59
  458.9 11.7 %cholesky.493 = f32[128,128]{1,0:T(8,128)S(1)} custom-call(f32[128,128]{1,0:T(8,128)S(1)} %cholesky.676), custom_call_target="Cholesky" | custom-call | tf_op jit(solution)/shard_map/jit(cholesky)/cholesky | solution.py:59
  471.4 9.8 %custom-call.72 = f32[1,128,128]{1,2,0:T(8,128)S(1)} custom-call(f32[1,128,128]{2,1,0:T(8,128)S(1)} %get-tuple-element.240), custom_call_target="InvertDiagBlocksLowerTriangular" | custom-call | tf_op jit(solution)/shard_map/jit(cholesky)/cholesky | solution.py:59
  482.4 3.3 convolution_subtract_fusion.2
  485.7 11.7 %cholesky.512 = f32[128,128]{1,0:T(8,128)S(1)} custom-call(f32[128,128]{1,0:T(8,128)S(1)} %cholesky.681), custom_call_target="Cholesky" | custom-call | tf_op jit(solution)/shard_map/jit(cholesky)/cholesky | solution.py:59
  498.2 9.8 %custom-call.73 = f32[1,128,128]{1,2,0:T(8,128)S(1)} custom-call(f32[1,128,128]{2,1,0:T(8,128)S(1)} %get-tuple-element.238), custom_call_target="InvertDiagBlocksLowerTriangular" | custom-call | tf_op jit(solution)/shard_map/jit(cholesky)/cholesky | solution.py:59
  509.2 3.2 convolution_subtract_fusion.3
  512.3 11.9 %cholesky.531 = f32[128,128]{1,0:T(8,128)S(1)} custom-call(f32[128,128]{1,0:T(8,128)S(1)} %cholesky.686), custom_call_target="Cholesky" | custom-call | tf_op jit(solution)/shard_map/jit(cholesky)/cholesky | solution.py:59
  525.0 9.8 %custom-call.74 = f32[1,128,128]{1,2,0:T(8,128)S(1)} custom-call(f32[1,128,128]{2,1,0:T(8,128)S(1)} %get-tuple-element.236), custom_call_target="InvertDiagBlocksLowerTriangular" | custom-call | tf_op jit(solution)/shard_map/jit(cholesky)/cholesky | solution.py:59
  535.9 3.1 convolution_subtract_fusion.4
  539.0 11.7 %cholesky.551 = f32[128,128]{1,0:T(8,128)S(1)} custom-call(f32[128,128]{1,0:T(8,128)S(1)} %cholesky.691), custom_call_target="Cholesky" | custom-call | tf_op jit(solution)/shard_map/jit(cholesky)/cholesky | solution.py:59
  551.5 9.8 %custom-call.75 = f32[1,128,128]{1,2,0:T(8,128)S(1)} custom-call(f32[1,128,128]{2,1,0:T(8,128)S(1)} %get-tuple-element.234), custom_call_target="InvertDiagBlocksLowerTriangular" | custom-call | tf_op jit(solution)/shard_map/jit(cholesky)/cholesky | solution.py:59
  565.4 11.7 %cholesky.571 = f32[128,128]{1,0:T(8,128)S(1)} custom-call(f32[128,128]{1,0:T(8,128)S(1)} %cholesky.696), custom_call_target="Cholesky" | custom-call | tf_op jit(solution)/shard_map/jit(cholesky)/cholesky | solution.py:59
  577.9 9.8 %custom-call.76 = f32[1,128,128]{1,2,0:T(8,128)S(1)} custom-call(f32[1,128,128]{2,1,0:T(8,128)S(1)} %get-tuple-element.232), custom_call_target="InvertDiagBlocksLowerTriangular" | custom-call | tf_op jit(solution)/shard_map/jit(cholesky)/cholesky | solution.py:59
  590.7 11.7 %cholesky.589 = f32[128,128]{1,0:T(8,128)S(1)} custom-call(f32[128,128]{1,0:T(8,128)S(1)} %convolution_subtract_fusion.41), custom_call_target="Cholesky" | custom-call | tf_op jit(solution)/shard_map/jit(cholesky)/cholesky | solution.py:59
  613.6 4.9 select_select_fusion
  618.5 28.2 %while.14 = (s32[]{:T(128)}, f32[1024,1024]{0,1:T(8,128)}, s32[8,2]{0,1:T(2,128)S(1)}, f32[8,128,128]{2,1,0:T(8,128)}, s32[]{:T(128)}) while((s32[]{:T(128)}, f32[1024,1024]{0,1:T(8,128)}, s32[8,2]{0,1:T(2,128)S(1)}, f32[8,128,128]{2,1,0:T(8,128)}, s32[]{:T(128)}) %tuple.152), condition=%wide.while_cond.clone.2, body=%wide.while_body.clone.2.sunk | while | flops 2 | bytes 393829 | solution.py:39
  646.6 79.5 %custom-call.93 = f32[8,128,128]{1,2,0:T(8,128)S(1)} custom-call(f32[8,128,128]{2,1,0:T(8,128)} %get-tuple-element.62), custom_call_target="InvertDiagBlocksLowerTriangular" | custom-call | tf_op jit(solution)/shard_map/triangular_solve/custom-call.16 | solution.py:39
  739.5 5.5 copy.134
  745.0 7.9 fusion
  754.8 3.4 fusion.333
  780.2 11.7 %cholesky.636 = f32[128,128]{1,0:T(8,128)S(1)} custom-call(f32[128,128]{1,0:T(8,128)S(1)} %fusion.231), custom_call_target="Cholesky" | custom-call | tf_op jit(solution)/shard_map/jit(cholesky)/cholesky | solution.py:69
  793.3 9.8 %custom-call.86 = f32[1,128,128]{1,2,0:T(8,128)S(1)} custom-call(f32[1,128,128]{2,1,0:T(8,128)S(1)} %fusion.207), custom_call_target="InvertDiagBlocksLowerTriangular" | custom-call | tf_op jit(solution)/shard_map/triangular_solve/custom-call.18 | solution.py:39
  817.4 3.4 fusion.334
  836.9 11.9 %cholesky.647 = f32[128,128]{1,0:T(8,128)S(1)} custom-call(f32[128,128]{1,0:T(8,128)S(1)} %fusion.229), custom_call_target="Cholesky" | custom-call | tf_op jit(solution)/shard_map/jit(cholesky)/cholesky | solution.py:69
  850.2 9.8 %custom-call.89 = f32[1,128,128]{1,2,0:T(8,128)S(1)} custom-call(f32[1,128,128]{2,1,0:T(8,128)S(1)} %fusion.208), custom_call_target="InvertDiagBlocksLowerTriangular" | custom-call | tf_op jit(solution)/shard_map/triangular_solve/custom-call.18 | solution.py:39
  874.1 3.9 fusion.335
  900.5 11.7 %cholesky.658 = f32[128,128]{1,0:T(8,128)S(1)} custom-call(f32[128,128]{1,0:T(8,128)S(1)} %fusion.227), custom_call_target="Cholesky" | custom-call | tf_op jit(solution)/shard_map/jit(cholesky)/cholesky | solution.py:69
  913.6 9.9 %custom-call.92 = f32[1,128,128]{1,2,0:T(8,128)S(1)} custom-call(f32[1,128,128]{2,1,0:T(8,128)S(1)} %fusion.209), custom_call_target="InvertDiagBlocksLowerTriangular" | custom-call | tf_op jit(solution)/shard_map/triangular_solve/custom-call.18 | solution.py:39
  (408 shorter events, 197.1 us)
Async XLA Ops:
  7.4 263.2 %all-reduce.7.cloned.1.call-start = ((), (), s32[]{:S(2)}) async-start(), calls=%async_computation.1 | async-start | bytes 16777216 | tf_op jit(solution)/shard_map/psum | solution.py:18
  34.3 15.2 %collective-permute-start = (f32[10,1024]{0,1:T(8,128)S(1)}, f32[10,1024]{0,1:T(8,128)S(1)}, u32[]{:S(2)}, u32[]{:S(2)}) collective-permute-start(f32[10,1024]{0,1:T(8,128)S(1)} %bitcast.438), channel_id=1, source_target_pairs={{1,0},{2,1},{3,2},{4,3},{5,4},{6,5},{7,6},{9,8},{10,9},{11,10},{12... | collective-permute-start | bytes 122888 | tf_op jit(solution)/shard_map/ppermute | solution.py:28
  55.6 215.0 %all-gather.5.cloned.1.call-start = ((), (), s32[]{:S(2)}) async-start(), calls=%async_computation | async-start | bytes 4210688 | tf_op jit(solution)/shard_map/all_gather | solution.py:94
  56.3 324.3 %all-reduce.9.cloned.1.call-start = ((), (), s32[]{:S(2)}) async-start(), calls=%async_computation.2 | async-start | bytes 16777216 | tf_op jit(solution)/shard_map/psum | solution.py:18
  399.9 2.0 copy-start.3
  439.8 14.4 %copy-start.8 = (f32[128,128]{0,1:T(8,128)S(1)}, f32[128,128]{0,1:T(8,128)}, u32[]{:S(2)}) copy-start(f32[128,128]{0,1:T(8,128)} %copy.119) | copy-start | bytes 196612
  613.6 4.9 copy-start.9
  752.9 1.9 copy-start
  763.3 0.8 copy-start.4
  764.0 0.7 copy-start.5
  806.7 10.7 %copy-start.1 = (f32[1024,1024]{1,0:T(8,128)S(1)}, f32[1024,1024]{1,0:T(8,128)}, u32[]{:S(2)}) copy-start(f32[1024,1024]{1,0:T(8,128)} %copy-done) | copy-start | bytes 12582916
  825.9 0.7 copy-start.6
  863.6 10.5 %copy-start.2 = (f32[1024,1024]{1,0:T(8,128)S(1)}, f32[1024,1024]{1,0:T(8,128)}, u32[]{:S(2)}) copy-start(f32[1024,1024]{1,0:T(8,128)} %copy-done) | copy-start | bytes 12582916
  885.9 13.6 %copy-start.7 = (f32[128,128]{0,1:T(8,128)S(1)}, f32[128,128]{0,1:T(8,128)}, u32[]{:S(2)}) copy-start(f32[128,128]{0,1:T(8,128)} %copy.183) | copy-start | bytes 196612
Sparse Core Ops, SparseCore 0:
  55.7 214.7 all-reduce.6
  273.0 107.6 all-reduce.8
Sparse Core Ops, SparseCore 1:
  59.7 142.1 all-gather.4
